TPU v7x, 512 devices: a whole 4x4x16 slice. The times are simulated.
512 devices in a mesh: region: 8 (over z_hi, x), blk: 64 (over y, z_lo, core).
Axes of the slice: x: 4, y: 4, z: 16 (z_hi: 2, z_lo: 8; z = z_hi * 8 + z_lo), core: 2. Of those that a mesh axis runs over, the one named last changes fastest.
Arguments:
- records: float32 [2048, 2048], P(('region', 'blk')), may hold values from -6 to 6
- starts: int32 [2048], P(('region', 'blk')), may hold values from 0 to 1024
- tapers: int32 [2048], P(('region', 'blk')), may hold values from 2 to 256
- pair_a: int32 [393216], P(('region', 'blk')), may hold values from 0 to 3
- pair_b: int32 [393216], P(('region', 'blk')), may hold values from 0 to 255
- pair_count: int32 [512], P(('region', 'blk')), may hold values from 192 to 768, as said below
- observed: float32 [393216, 512], P(('region', 'blk')), may hold values from -6 to 6
Outputs:
- correlations: float32 [393216, 512], P(('region', 'blk'))
- far_correlations: float32 [2048, 512], P(('region', 'blk'))
- adjoint: float32 [2048, 1024], P(('region', 'blk'))
Inputs may be any that keep to these rules, and one draw needn't show every extreme that they name: `pair_count`: device 0 has all 768 slots live.
All inputs are finite; a program needn't handle non-finite values.
Results may differ from a plain program's by a relative error of at most 0.0003.
Values sent between devices are 32-bit elements; how exact they have to be, the bound alone decides.
A program may use at most 64 MiB of HBM per device.

v0:
```python
import math
import jax
import jax.numpy as jnp
from jax import lax
from jax.sharding import PartitionSpec as P

WIN = 1024


def shifted(shard, axis, by):
    size = lax.axis_size(axis)
    return lax.ppermute(shard, axis, [(i, (i + by) % size) for i in range(size)])


def phase_table(rows, cols, length):
    product = rows[:, None] * cols[None, :] % length
    return product.astype(jnp.float32) * (2.0 * math.pi / length)


def taper_windows(records, starts, tapers):
    sample = jnp.arange(WIN, dtype=jnp.int32)
    picked = jnp.take_along_axis(records, starts[:, None] + sample[None, :], axis=1)
    lengths = tapers.astype(jnp.float32)[:, None]
    position = sample.astype(jnp.float32)[None, :]
    shape_fn = jnp.minimum(1.0, jnp.minimum((position + 1.0) / lengths, (WIN - position) / lengths))
    return picked * shape_fn * WIN ** (-0.25)


def to_spectra(windows):
    angle = phase_table(
        jnp.arange(WIN, dtype=jnp.int32), jnp.arange(WIN // 2, dtype=jnp.int32), WIN
    )
    real_part = jnp.dot(windows, jnp.cos(angle), precision=lax.Precision.HIGHEST)
    imag_part = jnp.dot(windows, -jnp.sin(angle), precision=lax.Precision.HIGHEST)
    return jnp.concatenate([real_part, imag_part], axis=1)


def bin_weights():
    bins = jnp.arange(WIN // 2, dtype=jnp.int32)
    weight = jnp.where(bins == 0, 1.0, 2.0).astype(jnp.float32) / WIN
    return jnp.concatenate([weight, weight])


def lag_index():
    return (jnp.arange(WIN // 2, dtype=jnp.int32) - WIN // 4) % WIN


def to_lags(cross_spec):
    angle = phase_table(jnp.arange(WIN // 2, dtype=jnp.int32), lag_index(), WIN)
    table = jnp.concatenate([jnp.cos(angle), -jnp.sin(angle)], axis=0)
    return jnp.dot(cross_spec * bin_weights()[None, :], table, precision=lax.Precision.HIGHEST)


def from_lags(residual):
    angle = phase_table(lag_index(), jnp.arange(WIN // 2, dtype=jnp.int32), WIN)
    table = jnp.concatenate([jnp.cos(angle), -jnp.sin(angle)], axis=1)
    return jnp.dot(residual, table, precision=lax.Precision.HIGHEST)


def to_time(source):
    half = WIN // 2
    angle = phase_table(jnp.arange(half, dtype=jnp.int32), jnp.arange(WIN, dtype=jnp.int32), WIN)
    weighted = source * bin_weights()[None, :]
    first = jnp.dot(weighted[:, :half], jnp.cos(angle), precision=lax.Precision.HIGHEST)
    second = jnp.dot(weighted[:, half:], jnp.sin(angle), precision=lax.Precision.HIGHEST)
    return (first - second) * (1.0 / 16.0)


def cross(left, right):
    half = WIN // 2
    left_r, left_i = (left[:, :half], left[:, half:])
    right_r, right_i = (right[:, :half], right[:, half:])
    return jnp.concatenate(
        [left_r * right_r + left_i * right_i, left_i * right_r - left_r * right_i], axis=1
    )


def times_plain(misfit, spec):
    half = WIN // 2
    mis_r, mis_i = (misfit[:, :half], misfit[:, half:])
    spec_r, spec_i = (spec[:, :half], spec[:, half:])
    return jnp.concatenate(
        [mis_r * spec_r - mis_i * spec_i, mis_r * spec_i + mis_i * spec_r], axis=1
    )


def times_conj(misfit, spec):
    half = WIN // 2
    mis_r, mis_i = (misfit[:, :half], misfit[:, half:])
    spec_r, spec_i = (spec[:, :half], spec[:, half:])
    return jnp.concatenate(
        [mis_r * spec_r + mis_i * spec_i, mis_r * spec_i - mis_i * spec_r], axis=1
    )


def body(records, starts, tapers, pair_a, pair_b, pair_count, observed):
    stations = records.shape[0]
    blocks = lax.axis_size("blk")
    slots = pair_a.shape[0]
    windows = taper_windows(records, starts, tapers)
    spectra = to_spectra(windows)
    group_spec = lax.all_gather(spectra, "blk", axis=0, tiled=True)
    prior = shifted(spectra, "region", 1)
    source_spec = jnp.take(spectra, pair_a, axis=0)
    target_spec = jnp.take(group_spec, pair_b, axis=0)
    live_rows = (jnp.arange(slots, dtype=jnp.int32) < pair_count[0]).astype(jnp.float32)[:, None]
    corr_raw = to_lags(cross(source_spec, target_spec))
    misfit = from_lags((corr_raw - observed) * live_rows)
    group_onehot = (
        jnp.arange(stations * blocks, dtype=jnp.int32)[:, None] == pair_b[None, :]
    ).astype(jnp.float32)
    remote_terms = jnp.dot(
        group_onehot, times_conj(misfit, source_spec), precision=lax.Precision.HIGHEST
    )
    own_onehot = (jnp.arange(stations, dtype=jnp.int32)[:, None] == pair_a[None, :]).astype(
        jnp.float32
    )
    local_terms = jnp.dot(
        own_onehot, times_plain(misfit, target_spec), precision=lax.Precision.HIGHEST
    )
    far_correlations = to_lags(cross(spectra, prior))
    returned = lax.psum_scatter(remote_terms, "blk", scatter_dimension=0, tiled=True)
    adjoint = to_time(local_terms + returned)
    return (corr_raw * live_rows, far_correlations, adjoint)


def solution(mesh):
    in_specs = (
        P(("region", "blk"), None),
        P(("region", "blk")),
        P(("region", "blk")),
        P(("region", "blk")),
        P(("region", "blk")),
        P(("region", "blk")),
        P(("region", "blk"), None),
    )
    out_specs = (P(("region", "blk"), None), P(("region", "blk"), None), P(("region", "blk"), None))
    return jax.shard_map(body, mesh=mesh, in_specs=in_specs, out_specs=out_specs, check_vma=False)
```

profile of v0, /device:TPU:1, one launch (start us, length us, event | category | flops | bytes accessed | tf_op | source)
XLA Modules:
  0.0 1073.0 jit_solution(7538603702445230818)
XLA Ops:
  7.2 0.0 copy-start
  7.2 0.0 all-gather.3.cloned.1.call-start
  7.2 0.7 fusion.78
  8.0 0.0 copy-done
  8.0 0.0 copy-start.10
  8.0 0.0 copy-start.9
  8.0 34.9 %gather_fusion.2 = f32[4096]{0:T(1024)S(1)} fusion(f32[4,2048]{1,0:T(4,128)S(1)} %copy-done, s32[4096]{0:T(1024)S(1)} %bitcast.13), kind=kCustom, calls=%fused_computation.2 | custom fusion | bytes 65536 | tf_op jit(solution)/shard_map/jit(take_along_axis)/gather | solution.py:22
  43.0 0.0 copy-done.10
  43.0 0.0 copy-done.9
  43.0 0.1 fusion.74
  43.1 8.9 fusion.27
  51.9 0.0 copy-start.8
  52.0 8.7 fusion.30
  60.7 0.6 pad_maximum_fusion.3
  61.3 0.0 all-gather.3.cloned.1.call-update
  61.3 0.2 all-reduce.3.cloned.1.call-start
  62.2 0.0 copy-done.8
  62.2 0.0 copy-start.7
  62.2 2.5 gather_fusion
  64.8 0.0 copy-done.7
  64.9 9.3 fusion.69
  74.2 1.9 broadcast_select_fusion.1
  76.1 111.2 %all-gather.3.cloned.1.call-done = f32[64,4,1024]{2,1,0:T(4,128)} async-done(((f32[1,4,1024]{2,1,0:T(4,128)}), f32[64,4,1024]{2,1,0:T(4,128)}) %all-gather.3.cloned.1.call-update) | async-done | bytes 1048592 | tf_op jit(solution)/shard_map/all_gather | solution.py:102
  187.3 1.6 reshape.148
  188.9 3.6 gather_fusion.1
  192.5 0.0 copy-start.1
  192.5 2.3 broadcast_select_fusion
  194.9 0.5 copy-done.1
  195.4 0.0 copy-start.2
  195.4 0.0 copy-start.3
  195.4 0.8 multiply_add_fusion.2
  196.2 0.4 copy-done.2
  196.6 0.3 copy-done.3
  196.9 0.0 copy-start.4
  196.9 0.0 copy-start.5
  196.9 0.0 copy-start.6
  196.9 6.2 broadcast_multiply_fusion
  203.2 0.0 copy-done.4
  203.2 0.0 copy-done.5
  203.2 0.0 copy-done.6
  203.2 5.3 fusion.17
  208.4 3.1 multiply_add_fusion
  211.5 3.0 fusion.7
  214.6 0.0 all-reduce.3.cloned.1.call-update
  214.6 3.1 collective-permute-start
  217.7 1.3 dynamic-slice
  219.6 10.3 collective-permute-done
  230.0 1.7 fusion.36
  231.7 812.9 %all-reduce.3.cloned.1.call-done = f32[256,1024]{1,0:T(8,128)} async-done(((f32[256,1024]{1,0:T(8,128)}), f32[256,1024]{1,0:T(8,128)}) %all-reduce.3.cloned.1.call-update) | async-done | bytes 1048592
  1044.5 3.0 fusion.49
  1047.5 9.0 fusion.21
  1056.5 9.7 fusion.43
  (15 shorter events, 0.1 us)
Async XLA Ops:
  7.2 0.8 copy-start
  7.2 180.1 %all-gather.3.cloned.1.call-start = ((), (), s32[]{:S(2)}) async-start(), calls=%async_computation | async-start | bytes 1064960 | tf_op jit(solution)/shard_map/all_gather | solution.py:102
  8.0 35.0 %copy-start.10 = (s32[4]{0:T(128)S(1)}, s32[4]{0:T(128)}, u32[]{:S(2)}) copy-start(s32[4]{0:T(128)} %param.9) | copy-start | bytes 52
  8.0 35.0 %copy-start.9 = (s32[4]{0:T(128)S(1)}, s32[4]{0:T(128)}, u32[]{:S(2)}) copy-start(s32[4]{0:T(128)} %param.8) | copy-start | bytes 52
  51.9 10.2 copy-start.8
  61.3 983.2 %all-reduce.3.cloned.1.call-start = ((), (), s32[]{:S(2)}) async-start(), calls=%async_computation.1 | async-start | bytes 2097152
  62.2 2.6 copy-start.7
  192.5 2.8 copy-start.1
  195.4 1.2 copy-start.2
  195.4 1.5 copy-start.3
  196.9 6.3 copy-start.4
  196.9 6.3 copy-start.5
  196.9 6.3 copy-start.6
  214.6 15.4 %collective-permute-start = (f32[4,1024]{1,0:T(4,128)S(1)}, f32[4,1024]{1,0:T(4,128)S(1)}, u32[]{:S(2)}, u32[]{:S(2)}) collective-permute-start(f32[4,1024]{1,0:T(4,128)S(1)} %get-tuple-element.13), channel_id=1, source_target_pairs={{0,64},{64,128},{128,192},{192,256},{256,320},{320,384},{384,448},... | collective-permute-start | bytes 49160 | tf_op jit(solution)/shard_map/ppermute | solution.py:12
Sparse Core Ops, SparseCore 0:
  61.4 125.8 all-gather.2
  214.7 829.7 all-reduce.2
where the time goes:
time: 1070 us
  waiting for transfers between devices  934 us (87%)
  matrix products  55.5 us (5%)
  local copies, waits for them, and re-layouts  45.2 us (4%)
  other arithmetic  19 us (2%)
  between operations  15.6 us (1%)
    unnamed x3, waiting for transfers between devices  813 us
    all_gather x1, waiting for transfers between devices, body(): group_spec = lax.all_gather(spectra, 'blk', axis=0, tiled=True)  111 us
    gather x2, local copies, waits for them, and re-layouts, taper_windows(): jnp.take_along_axis(records, starts[:, None] + sample[None, :], axis=1)  34.9 us
  transfers between devices with their start and end apart: 3, of which 3 were waited for; matrix products, arithmetic and copies ran while one was open for 2% of the time, Pallas kernels for 0%

commit v1 on v0

--- a/solution.py
+++ b/solution.py
@@ -99,7 +99,9 @@
     slots = pair_a.shape[0]
     windows = taper_windows(records, starts, tapers)
     spectra = to_spectra(windows)
-    group_spec = lax.all_gather(spectra, "blk", axis=0, tiled=True)
+    group_spec = jnp.concatenate(
+        lax.all_to_all(jnp.stack([spectra] * lax.axis_size("blk")), "blk", 0, 0), axis=0
+    )
     prior = shifted(spectra, "region", 1)
     source_spec = jnp.take(spectra, pair_a, axis=0)
     target_spec = jnp.take(group_spec, pair_b, axis=0)

time: 1070 us -> 1020 us (0.953)
  waiting for transfers between devices: 934 us -> 860 us
  starting transfers between devices: 3.36 us -> 20.7 us
    all_gather x1 -> x0, waiting for transfers between devices: 111 us -> none  [body(): group_spec = lax.all_gather(spectra, 'blk', axis=0, tiled=True)]
    all_to_all x0 -> x1, waiting for transfers between devices: none -> 36.4 us  [body(): lax.all_to_all(jnp.stack([spectra] * lax.axis_size('blk')), 'blk', 0, 0)]
    all_to_all x0 -> x1, starting transfers between devices: none -> 17.4 us  [body(): lax.all_to_all(jnp.stack([spectra] * lax.axis_size('blk')), 'blk', 0, 0)]
    unnamed x3 -> x2, waiting for transfers between devices: 813 us -> 814 us
where the time goes in v1:
time: 1020 us
  waiting for transfers between devices  860 us (84%)
  matrix products  55.5 us (5%)
  local copies, waits for them, and re-layouts  46.5 us (5%)
  starting transfers between devices  20.7 us (2%)
  other arithmetic  18.4 us (2%)
  between operations  15.6 us (2%)
    unnamed x2, waiting for transfers between devices  814 us
    all_to_all x1, waiting for transfers between devices, body(): lax.all_to_all(jnp.stack([spectra] * lax.axis_size('blk')), 'blk', 0, 0)  36.4 us
    gather x2, local copies, waits for them, and re-layouts, taper_windows(): jnp.take_along_axis(records, starts[:, None] + sample[None, :], axis=1)  34.9 us
  transfers between devices with their start and end apart: 3, of which 3 were waited for; matrix products, arithmetic and copies ran while one was open for 2% of the time, Pallas kernels for 0%

profile of v1, /device:TPU:1, one launch (start us, length us, event | category | flops | bytes accessed | tf_op | source)
XLA Modules:
  0.0 1017.1 jit_solution(12237314966877421504)
XLA Ops:
  7.2 0.0 copy-start
  7.2 0.7 fusion.78
  7.9 0.0 copy-done
  8.0 0.0 copy-start.10
  8.0 0.0 copy-start.9
  8.0 34.9 %gather_fusion.2 = f32[4096]{0:T(1024)S(1)} fusion(f32[4,2048]{1,0:T(4,128)S(1)} %copy-done, s32[4096]{0:T(1024)S(1)} %bitcast.11), kind=kCustom, calls=%fused_computation.2 | custom fusion | bytes 65536 | tf_op jit(solution)/shard_map/jit(take_along_axis)/gather | solution.py:22
  42.9 0.0 copy-done.10
  42.9 0.0 copy-done.9
  43.0 0.1 fusion.74
  43.1 8.9 fusion.27
  51.9 8.7 fusion.30
  60.6 0.0 copy-start.8
  60.6 1.2 stack.2
  61.9 17.4 %all-to-all-start = ((f32[64,4,1024]{2,1,0:T(4,128)}), f32[64,4,1024]{2,1,0:T(4,128)}, u32[]{:S(2)}, u32[]{:S(2)}) async-start(f32[64,4,1024]{2,1,0:T(4,128)} %stack.2), calls=%async_computation | async-start | bytes 2097152 | tf_op jit(solution)/shard_map/all_to_all | solution.py:103
  79.3 0.2 all-reduce.3.cloned.1.call-start
  80.2 0.0 copy-done.8
  80.2 0.0 copy-start.7
  80.2 2.5 gather_fusion
  82.7 0.0 copy-done.7
  82.8 9.3 fusion.69
  92.2 1.9 broadcast_select_fusion.1
  94.1 36.4 %all-to-all-done = f32[64,4,1024]{2,1,0:T(4,128)} async-done(((f32[64,4,1024]{2,1,0:T(4,128)}), f32[64,4,1024]{2,1,0:T(4,128)}, u32[]{:S(2)}, u32[]{:S(2)}) %all-to-all-start) | async-done | bytes 1048608 | tf_op jit(solution)/shard_map/all_to_all | solution.py:103
  130.5 1.6 reshape.128
  132.1 3.7 gather_fusion.1
  135.7 0.0 copy-start.1
  135.7 2.3 broadcast_select_fusion
  138.1 0.5 copy-done.1
  138.6 0.0 copy-start.2
  138.6 0.0 copy-start.3
  138.6 0.8 multiply_add_fusion.2
  139.4 0.4 copy-done.2
  139.8 0.3 copy-done.3
  140.1 0.0 copy-start.4
  140.1 0.0 copy-start.5
  140.1 0.0 copy-start.6
  140.1 6.2 broadcast_multiply_fusion
  146.4 0.0 copy-done.4
  146.4 0.0 copy-done.5
  146.4 0.0 copy-done.6
  146.4 5.3 fusion.17
  151.6 3.1 multiply_add_fusion
  154.8 3.0 fusion.7
  157.8 0.0 all-reduce.3.cloned.1.call-update
  157.8 3.1 collective-permute-start
  160.9 1.3 dynamic-slice
  162.8 10.3 %collective-permute-done = f32[4,1024]{1,0:T(4,128)S(1)} collective-permute-done((f32[4,1024]{1,0:T(4,128)S(1)}, f32[4,1024]{1,0:T(4,128)S(1)}, u32[]{:S(2)}, u32[]{:S(2)}) %collective-permute-start) | collective-permute-done | bytes 16416 | tf_op jit(solution)/shard_map/ppermute | solution.py:12
  173.1 1.7 fusion.36
  174.8 813.8 %all-reduce.3.cloned.1.call-done = f32[256,1024]{1,0:T(8,128)} async-done(((f32[256,1024]{1,0:T(8,128)}), f32[256,1024]{1,0:T(8,128)}) %all-reduce.3.cloned.1.call-update) | async-done | bytes 1048592
  988.6 3.0 fusion.49
  991.6 9.0 fusion.21
  1000.6 9.7 fusion.43
  (16 shorter events, 0.1 us)
Async XLA Ops:
  7.2 0.8 copy-start
  8.0 35.0 %copy-start.10 = (s32[4]{0:T(128)S(1)}, s32[4]{0:T(128)}, u32[]{:S(2)}) copy-start(s32[4]{0:T(128)} %param.9) | copy-start | bytes 52
  8.0 35.0 %copy-start.9 = (s32[4]{0:T(128)S(1)}, s32[4]{0:T(128)}, u32[]{:S(2)}) copy-start(s32[4]{0:T(128)} %param.8) | copy-start | bytes 52
  60.6 19.5 %copy-start.8 = (s32[768]{0:T(1024)S(1)}, s32[768]{0:T(1024)}, u32[]{:S(2)}) copy-start(s32[768]{0:T(1024)} %param.10) | copy-start | bytes 9220
  61.9 68.6 %all-to-all-start = ((f32[64,4,1024]{2,1,0:T(4,128)}), f32[64,4,1024]{2,1,0:T(4,128)}, u32[]{:S(2)}, u32[]{:S(2)}) async-start(f32[64,4,1024]{2,1,0:T(4,128)} %stack.2), calls=%async_computation | async-start | bytes 2097152 | tf_op jit(solution)/shard_map/all_to_all | solution.py:103
  79.3 909.3 %all-reduce.3.cloned.1.call-start = ((), (), s32[]{:S(2)}) async-start(), calls=%async_computation.1 | async-start | bytes 2097152
  80.2 2.6 copy-start.7
  135.7 2.8 copy-start.1
  138.6 1.2 copy-start.2
  138.6 1.5 copy-start.3
  140.1 6.3 copy-start.4
  140.1 6.3 copy-start.5
  140.1 6.3 copy-start.6
  157.8 15.3 %collective-permute-start = (f32[4,1024]{1,0:T(4,128)S(1)}, f32[4,1024]{1,0:T(4,128)S(1)}, u32[]{:S(2)}, u32[]{:S(2)}) collective-permute-start(f32[4,1024]{1,0:T(4,128)S(1)} %pad_maximum_fusion.3), channel_id=1, source_target_pairs={{0,64},{64,128},{128,192},{192,256},{256,320},{320,384},{384,448},... | collective-permute-start | bytes 49160 | tf_op jit(solution)/shard_map/ppermute | solution.py:12
Sparse Core Ops, SparseCore 0:
  157.9 830.6 all-reduce.2
